TPU v7x, 32 devices: a whole 2x2x4 slice. The times are simulated.
32 devices in a mesh: ctx: 8 (over y, x, core), exp: 4 (over z).
Axes of the slice: x: 2, y: 2, z: 4, core: 2. Of those that a mesh axis runs over, the one named last changes fastest.
Arguments:
- conv_input: bfloat16 [1024, 4096], P('ctx', 'exp'), may hold values from -6 to 6
- conv_weight: float32 [4, 4096], P(None, 'exp'), may hold values from -3 to 3
- b_proj: bfloat16 [1024, 128], P('ctx'), may hold values from -0.5 to 0.5
- c_proj: bfloat16 [1024, 128], P('ctx'), may hold values from -0.29882812 to 0.29882812
- log_decay: float32 [64, 1024], P('exp', 'ctx'), may hold values from -1 to 0
- skip_gain: float32 [64], P('exp'), may hold values from 0.5 to 1.5
- grad_in: bfloat16 [1024, 4096], P('ctx', 'exp'), may hold values from -6 to 6
- norm_gain: float32 [4096], replicated, may hold values from 0.1 to 1.9
- expert_ids: int32 [1024, 2], P('ctx'), may hold values from 0 to 3, all different within a row; in each aligned block of 32 rows (0 to 31, 32 to 63, ...) at most 24 rows name the same one
- expert_weights: float32 [1024, 2], P('ctx'), may hold values from 0.1 to 1
- up_weight: bfloat16 [4, 4096, 12288], P('exp', None, 'ctx'), may hold values from -0.09375 to 0.09375
- down_weight: bfloat16 [4, 12288, 4096], P('exp', 'ctx'), may hold values from -0.0546875 to 0.0546875
Outputs:
- moe_out: bfloat16 [1024, 4096], P('ctx', 'exp')
- grad_conv: float32 [1024, 4096], P('ctx', 'exp')
Inputs may be any that keep to these rules, and one draw needn't show every extreme that they name: `expert_ids`: each token names 2 different experts; in each aligned block of 32 tokens no expert is named more than 24 times.
All inputs are finite; a program needn't handle non-finite values.
Results may differ from a plain program's by a relative error of at most 0.018.
Values may be sent and summed in bfloat16 or wider, within the bound.
No kernel may reach another device: no remote copies, remote signals or barrier semaphores. Data moves between devices by JAX's collectives and lax.ppermute only.
A program may use at most 128 MiB of HBM per device.

v0:
```python
import jax
import jax.numpy as jnp
from jax import lax
from jax.sharding import PartitionSpec as P

CONV = 4
TOPK = 2
HIGHEST = lax.Precision.HIGHEST
EPSILON = 1e-06


def passed_along(block, axis, distance):
    devices = range(lax.axis_size(axis))
    route = [(i - distance, i) for i in devices if i - distance in devices]
    return lax.ppermute(block, axis, route)


def prefix(x, axis, combine, identity, reverse):
    size, mine = (lax.axis_size(axis), lax.axis_index(axis))
    everything = jax.tree.map(
        lambda part, kind: lax.all_gather(part.astype(kind), axis), x, (jnp.bfloat16, jnp.bfloat16)
    )
    start = jax.tree.map(
        lambda part, zero: jnp.broadcast_to(jnp.asarray(zero, part.dtype), part.shape), x, identity
    )

    def turn(k, before):
        at = size - 1 - k if reverse else k
        reached = at > mine if reverse else at < mine
        new = combine(
            before, jax.tree.map(lambda part, own: part[at].astype(own.dtype), everything, x)
        )
        return jax.tree.map(lambda a, b: jnp.where(reached, a, b), new, before)

    return lax.fori_loop(0, size, turn, start)


def combine_state(earlier, later):
    return (earlier[0] * later[0], later[0][:, None, None] * earlier[1] + later[1])


def conv_mix(extended, conv_weight):
    rows_out = extended.shape[0] - conv_weight.shape[0] + 1
    total = jnp.zeros((rows_out, extended.shape[1]), jnp.float32)
    for offset in range(conv_weight.shape[0]):
        total = total + conv_weight[offset][None, :] * extended[offset : offset + rows_out]
    return jax.nn.silu(total).astype(jnp.bfloat16)


def block_terms(decay_block, b_raw, c_raw):
    totals = jnp.cumsum(decay_block, axis=1)
    rows_here = totals.shape[1]
    causal = jnp.arange(rows_here)[:, None] >= jnp.arange(rows_here)[None, :]
    spread = jnp.where(causal[None], totals[:, :, None] - totals[:, None, :], 0.0)
    kernel = (
        jnp.where(causal[None], jnp.exp(spread), 0.0)
        * jnp.dot(c_raw, b_raw.T, preferred_element_type=jnp.float32)[None]
    )
    to_end = jnp.exp(totals[:, -1:] - totals)
    return (totals, kernel, to_end)


def normalize(rows_in, norm_gain):
    values = rows_in.astype(jnp.float32)
    scale = lax.rsqrt(jnp.mean(values * values, axis=1, keepdims=True) + EPSILON)
    return (values * scale * norm_gain[None, :]).astype(jnp.bfloat16)


def route_matrix(chosen_ids, slots_each, experts):
    pairs = chosen_ids.reshape(-1)
    onehot = (pairs[:, None] == jnp.arange(experts, dtype=jnp.int32)[None, :]).astype(jnp.int32)
    ranks = jnp.sum((jnp.cumsum(onehot, axis=0) - 1) * onehot, axis=1)
    target = pairs * slots_each + ranks
    return (jnp.arange(experts * slots_each, dtype=jnp.int32)[:, None] == target[None, :]).astype(
        jnp.bfloat16
    )


def gather_back(dispatch, returned, weights):
    values = jnp.einsum("sp,sc->pc", dispatch, returned, preferred_element_type=jnp.float32)
    values = values.reshape(weights.shape[0], weights.shape[1], returned.shape[1])
    return jnp.sum(weights[:, :, None] * values, axis=1).astype(jnp.bfloat16)


def expert_block(rows_in, up_weight, down_weight):
    up_local = up_weight[0]
    down_local = down_weight[0]
    hidden = jax.nn.silu(
        jnp.dot(
            lax.all_gather(rows_in, "ctx", axis=0, tiled=True),
            up_local,
            preferred_element_type=jnp.float32,
        )
    ).astype(jnp.bfloat16)
    summed = lax.psum_scatter(
        jnp.dot(hidden, down_local, preferred_element_type=jnp.float32).astype(jnp.bfloat16),
        "ctx",
        scatter_dimension=0,
        tiled=True,
    )
    return summed


def shards(
    conv_input,
    conv_weight,
    b_proj,
    c_proj,
    log_decay,
    skip_gain,
    grad_in,
    norm_gain,
    expert_ids,
    expert_weights,
    up_weight,
    down_weight,
):
    tok_rows = conv_input.shape[0]
    heads_here = log_decay.shape[0]
    head_size = conv_input.shape[1] // heads_here
    rim_rows = passed_along(conv_input[tok_rows - (CONV - 1) :], "ctx", 1)
    extended = jnp.concatenate(
        [rim_rows.astype(jnp.float32), conv_input.astype(jnp.float32)], axis=0
    )
    mixed_in = conv_mix(extended, conv_weight)
    inputs_block = mixed_in.astype(jnp.float32).reshape(tok_rows, heads_here, head_size)
    b_block = b_proj.astype(jnp.float32)
    c_block = c_proj.astype(jnp.float32)
    grad_block = grad_in.astype(jnp.float32).reshape(tok_rows, heads_here, head_size)
    totals, kernel, to_end = block_terms(log_decay, b_proj, c_proj)
    through = jnp.exp(totals[:, -1])
    local_state = jnp.einsum("hs,shp,sn->hpn", to_end, inputs_block, b_block, precision=HIGHEST)
    local_grad = jnp.einsum(
        "ht,thp,tn->hpn", jnp.exp(totals), grad_block, c_block, precision=HIGHEST
    )
    zero_state = jnp.zeros_like(local_state)
    ones_heads = jnp.ones_like(through)
    carry_state = prefix(
        (through, local_state), "ctx", combine_state, (ones_heads, zero_state), False
    )[1]
    carry_grad = prefix(
        (through, local_grad), "ctx", combine_state, (ones_heads, zero_state), True
    )[1]
    inner = jnp.einsum("hts,shp->thp", kernel, inputs_block, precision=HIGHEST)
    carried = jnp.exp(totals).T[:, :, None] * jnp.einsum(
        "hpn,tn->thp", carry_state, c_block, precision=HIGHEST
    )
    output = inner + carried + skip_gain[None, :, None] * inputs_block
    ssd_out = output.reshape(tok_rows, heads_here * head_size).astype(jnp.bfloat16)
    grad_inner = jnp.einsum("hts,thp->shp", kernel, grad_block, precision=HIGHEST)
    grad_carried = to_end.T[:, :, None] * jnp.einsum(
        "hpn,sn->shp", carry_grad, b_block, precision=HIGHEST
    )
    grad_conv = (grad_inner + grad_carried + skip_gain[None, :, None] * grad_block).reshape(
        tok_rows, heads_here * head_size
    )
    experts = lax.axis_size("exp")
    most_rows = 3 * TOPK * tok_rows // (2 * experts * experts)
    share = tok_rows // experts
    token_view = lax.all_to_all(ssd_out, "exp", split_axis=0, concat_axis=1, tiled=True)
    normed = normalize(token_view, norm_gain)
    first_row = lax.axis_index("exp") * share
    my_ids = lax.dynamic_slice_in_dim(expert_ids, first_row, share, 0)
    my_weights = lax.dynamic_slice_in_dim(expert_weights, first_row, share, 0)
    dispatch = route_matrix(my_ids, most_rows, experts)
    outgoing = jnp.dot(
        dispatch, jnp.repeat(normed, TOPK, axis=0), preferred_element_type=jnp.float32
    ).astype(jnp.bfloat16)
    incoming = lax.all_to_all(
        outgoing.reshape(experts, most_rows, normed.shape[1]),
        "exp",
        split_axis=0,
        concat_axis=0,
        tiled=True,
    )
    results = expert_block(
        incoming.reshape(experts * most_rows, normed.shape[1]), up_weight, down_weight
    )
    returned = lax.all_to_all(
        results.reshape(experts, most_rows, normed.shape[1]),
        "exp",
        split_axis=0,
        concat_axis=0,
        tiled=True,
    )
    combined = gather_back(
        dispatch, returned.reshape(experts * most_rows, normed.shape[1]), my_weights
    )
    moe_out = lax.all_to_all(combined, "exp", split_axis=1, concat_axis=0, tiled=True)
    return (moe_out, grad_conv)


def solution(mesh):
    placed = (
        P("ctx", "exp"),
        P(None, "exp"),
        P("ctx", None),
        P("ctx", None),
        P("exp", "ctx"),
        P("exp"),
        P("ctx", "exp"),
        P(),
        P("ctx", None),
        P("ctx", None),
        P("exp", None, "ctx"),
        P("exp", "ctx", None),
    )
    return jax.shard_map(
        shards,
        mesh=mesh,
        in_specs=placed,
        out_specs=(P("ctx", "exp"), P("ctx", "exp")),
        check_vma=False,
    )
```

profile of v0, /device:TPU:0, one launch (start us, length us, event | category | flops | bytes accessed | tf_op | source)
XLA Modules:
  0.0 299.9 jit_solution(15138509072731504501)
XLA Ops:
  7.2 0.7 slice.29
  8.0 2.3 collective-permute-start
  10.3 0.9 fusion.53
  11.2 1.0 reduce_window_sum.23
  12.5 1.0 convert_element_type.132
  13.5 0.3 multiply_convert_fusion.2
  14.0 1.9 convolution_convert_fusion.2
  15.9 1.2 dynamic-slice
  18.0 0.2 dynamic-update-slice
  18.3 14.5 %all-reduce = bf16[128]{0:T(256)(128)(2,1)S(1)} all-reduce(bf16[128]{0:T(256)(128)(2,1)S(1)} %dynamic-update-slice), channel_id=2, replica_groups=mesh['ctx'=8,'exp'=4] {'ctx'}, use_global_device_ids=true, to_apply=%add | all-reduce | flops 128 | bytes 512
  32.8 0.8 constant_dynamic-slice_fusion
  33.8 0.9 fusion.54
  34.8 11.8 %all-gather.9.cloned.1.call-done = bf16[128,64,128]{2,1,0:T(8,128)(2,1)} async-done(((bf16[16,64,128]{2,1,0:T(8,128)(2,1)}), bf16[128,64,128]{2,1,0:T(8,128)(2,1)}) %all-gather.9.cloned.1.call-update) | async-done | bytes 2097168 | tf_op jit(solution)/shard_map/all_gather | solution.py:21
  46.6 9.1 %while.30 = (s32[]{:T(128)}, f32[16,64,128]{2,1,0:T(8,128)S(1)}, s32[]{:T(128)}, bf16[8,16]{1,0:T(8,128)(2,1)S(1)}, bf16[8,16,64,128]{3,2,1,0:T(8,128)(2,1)}, /*index=5*/s32[]{:T(128)}, s32[]{:T(128)}) while((s32[]{:T(128)}, f32[16,64,128]{2,1,0:T(8,128)S(1)}, s32[]{:T(128)}, bf16[8,16]{1,0:T(8,128)(2,1)S(1)}, ...), condition=%wide.region_4.5_spmd.clone, body=%wide.region_3.4_spmd.clone.sunk | while | flops 655380 | bytes 1310985 | solution.py:35
  46.6 1.1 fusion.66
  47.7 1.1 fusion.66
  48.8 1.1 fusion.66
  50.0 1.1 fusion.66
  51.1 1.1 fusion.66
  52.3 1.1 fusion.66
  53.4 1.1 fusion.66
  54.5 1.1 fusion.66
  55.6 0.4 fusion.18
  56.0 1.3 fusion.20
  57.4 0.4 copy.35
  57.8 1.1 convert_element_type.138
  58.8 4.6 %all-to-all-start = ((bf16[4,32,1024]{2,1,0:T(8,128)(2,1)}), bf16[4,32,1024]{2,1,0:T(8,128)(2,1)S(1)}, u32[]{:S(2)}, u32[]{:S(2)}) async-start(bf16[4,32,1024]{2,1,0:T(8,128)(2,1)} %convert_element_type.138), calls=%async_computation | async-start | bytes 524288 | tf_op jit(solution)/shard_map/all_to_all | solution.py:160
  63.8 8.9 %all-to-all-done = bf16[4,32,1024]{2,1,0:T(8,128)(2,1)S(1)} async-done(((bf16[4,32,1024]{2,1,0:T(8,128)(2,1)}), bf16[4,32,1024]{2,1,0:T(8,128)(2,1)S(1)}, u32[]{:S(2)}, u32[]{:S(2)}) %all-to-all-start) | async-done | bytes 262176 | tf_op jit(solution)/shard_map/all_to_all | solution.py:160
  73.2 0.5 broadcast_in_dim.50
  73.9 0.3 convolution_convert_fusion
  74.2 22.0 %all_to_all.36 = bf16[4,24,4096]{2,1,0:T(8,128)(2,1)} all-to-all(bf16[4,24,4096]{2,1,0:T(8,128)(2,1)S(1)} %bitcast.106), channel_id=1, replica_groups=mesh['ctx'=8,'exp'=4] {'exp'}, dimensions={0} | all-to-all | bytes 1572864 | tf_op jit(solution)/shard_map/all_to_all | solution.py:169
  96.2 0.2 reduce-scatter.2.cloned.1.call-start
  96.5 43.6 %all-gather.7.cloned.1.call-done = bf16[768,4096]{1,0:T(8,128)(2,1)} async-done(((bf16[96,4096]{1,0:T(8,128)(2,1)}), bf16[768,4096]{1,0:T(8,128)(2,1)}) %all-gather.7.cloned.1.call-update) | async-done | bytes 6291472 | tf_op jit(solution)/shard_map/all_gather | solution.py:90
  140.1 30.9 %fusion.6 = bf16[768,4096]{1,0:T(8,128)(2,1)} fusion(bf16[1,1536,4096]{2,1,0:T(8,128)(2,1)} %param.27, bf16[768,4096]{1,0:T(8,128)(2,1)} %all-gather.7.cloned.1.call-done, bf16[1,4096,1536]{2,1,0:T(8,128)(2,1)} %param.26), kind=kOutput, calls=%fused_computation.10 | convolution fusion | flops 19336396800 | bytes 37748736 | tf_op jit(solution)/shard_map/dot_general | solution.py:96
  171.1 0.8 copy-done.2
  172.2 1.1 convolution_convert_fusion.1
  173.5 59.4 %reduce-scatter.2.cloned.1.call-done = bf16[96,4096]{1,0:T(8,128)(2,1)} async-done(((bf16[768,4096]{1,0:T(8,128)(2,1)}), bf16[96,4096]{1,0:T(8,128)(2,1)}) %reduce-scatter.2.cloned.1.call-update) | async-done | bytes 786448 | tf_op jit(solution)/shard_map/reduce_scatter | solution.py:95
  232.9 4.6 %all-to-all-start.2 = ((bf16[4,24,4096]{2,1,0:T(8,128)(2,1)}), bf16[4,24,4096]{2,1,0:T(8,128)(2,1)S(1)}, u32[]{:S(2)}, u32[]{:S(2)}) async-start(bf16[4,24,4096]{2,1,0:T(8,128)(2,1)} %bitcast.116), calls=%async_computation.3 | async-start | bytes 1572864 | tf_op jit(solution)/shard_map/all_to_all | solution.py:179
  237.5 25.8 %all-gather.11.cloned.1.call-done = bf16[128,64,128]{2,1,0:T(8,128)(2,1)} async-done(((bf16[16,64,128]{2,1,0:T(8,128)(2,1)}), bf16[128,64,128]{2,1,0:T(8,128)(2,1)}) %all-gather.11.cloned.1.call-update) | async-done | bytes 2097168 | tf_op jit(solution)/shard_map/all_gather | solution.py:21
  263.3 14.4 %while.31 = (s32[]{:T(128)}, f32[16,64,128]{2,1,0:T(8,128)S(1)}, s32[]{:T(128)}, bf16[8,16]{1,0:T(8,128)(2,1)}, bf16[8,16,64,128]{3,2,1,0:T(8,128)(2,1)}, /*index=5*/s32[]{:T(128)}, s32[]{:T(128)}, s32[]{:T(128)}, s32[]{:T(128)}) while((s32[]{:T(128)}, f32[16,64,128]{2,1,0:T(8,128)S(1)}, s32[]{:T(128)}, bf16[8,16]{1,0:T(8,128)(2,1)}, ...), condition=%wide.region_9.10_spmd.clone, body=%wide.region_8.9_spmd.clone.sunk | while | flops 655384 | bytes 1311047 | solution.py:35
  263.3 0.7 bitcast_convert_fusion.5
  264.0 1.1 fusion.67
  265.1 0.7 bitcast_convert_fusion.5
  265.8 1.1 fusion.67
  266.9 0.7 bitcast_convert_fusion.5
  267.6 1.1 fusion.67
  268.7 0.7 bitcast_convert_fusion.5
  269.4 1.1 fusion.67
  270.5 0.7 bitcast_convert_fusion.5
  271.2 1.1 fusion.67
  272.3 0.7 bitcast_convert_fusion.5
  273.0 1.1 fusion.67
  274.1 0.7 bitcast_convert_fusion.5
  274.8 1.1 fusion.67
  275.9 0.7 bitcast_convert_fusion.5
  276.6 1.1 fusion.67
  277.7 0.3 fusion.13
  278.0 0.7 copy.46
  278.7 4.6 %all-to-all-start.3 = ((bf16[32,4,1024]{2,0,1:T(8,128)(2,1)}), bf16[32,4,1024]{2,0,1:T(8,128)(2,1)S(1)}, u32[]{:S(2)}, u32[]{:S(2)}) async-start(bf16[32,4,1024]{2,0,1:T(8,128)(2,1)} %bitcast.95), calls=%async_computation.4 | async-start | bytes 524288 | tf_op jit(solution)/shard_map/all_to_all | solution.py:189
  283.3 0.4 fusion.19
  283.7 0.9 fusion.15
  284.6 1.0 copy.40
  285.6 7.0 %all-to-all-done.3 = bf16[32,4,1024]{2,0,1:T(8,128)(2,1)S(1)} async-done(((bf16[32,4,1024]{2,0,1:T(8,128)(2,1)}), bf16[32,4,1024]{2,0,1:T(8,128)(2,1)S(1)}, u32[]{:S(2)}, u32[]{:S(2)}) %all-to-all-start.3) | async-done | bytes 262176 | tf_op jit(solution)/shard_map/all_to_all | solution.py:189
  292.6 0.7 copy.61
  (82 shorter events, 2.5 us)
Async XLA Ops:
  7.2 26.7 %copy-start = (bf16[128,128]{1,0:T(8,128)(2,1)S(1)}, bf16[128,128]{1,0:T(8,128)(2,1)}, u32[]{:S(2)}) copy-start(bf16[128,128]{1,0:T(8,128)(2,1)} %param.19) | copy-start | bytes 98308
  7.2 48.9 %copy-start.18 = (f32[16]{0:T(128)S(1)}, f32[16]{0:T(128)}, u32[]{:S(2)}) copy-start(f32[16]{0:T(128)} %param.21) | copy-start | bytes 196
  7.2 39.4 %all-gather.9.cloned.1.call-start = ((), (), s32[]{:S(2)}) async-start(), calls=%async_computation.7 | async-start | bytes 2359296 | tf_op jit(solution)/shard_map/all_gather | solution.py:21
  8.0 5.5 %collective-permute-start = (bf16[3,1024]{1,0:T(4,128)(2,1)S(1)}, bf16[3,1024]{1,0:T(4,128)(2,1)S(1)}, u32[]{:S(2)}, u32[]{:S(2)}) collective-permute-start(bf16[3,1024]{1,0:T(4,128)(2,1)S(1)} %slice.29), channel_id=1, source_target_pairs={{0,4},{4,8},{8,12},{12,16},{16,20},{20,24},{24,28},{1,5},{5,9},{9,... | collective-permute-start | bytes 18440 | tf_op jit(solution)/shard_map/ppermute | solution.py:15
  12.2 45.1 %copy-start.3 = (f32[16,128]{1,0:T(8,128)}, f32[16,128]{1,0:T(8,128)S(1)}, u32[]{:S(2)}) copy-start(f32[16,128]{1,0:T(8,128)S(1)} %reduce_window_sum.23) | copy-start | bytes 24580
  12.4 3.5 %copy-start.5 = (f32[128,16]{0,1:T(8,128)}, f32[128,16]{0,1:T(8,128)S(1)}, u32[]{:S(2)}) copy-start(f32[128,16]{0,1:T(8,128)S(1)} %get-tuple-element.299) | copy-start | bytes 24580
  12.4 44.9 %copy-start.7 = (f32[128,16]{0,1:T(8,128)}, f32[128,16]{0,1:T(8,128)S(1)}, u32[]{:S(2)}) copy-start(f32[128,16]{0,1:T(8,128)S(1)} %get-tuple-element.298) | copy-start | bytes 24580
  33.8 29.8 %copy-start.12 = (pred[128,128]{1,0:T(8,128)(4,1)}, pred[128,128]{1,0:T(8,128)(4,1)S(1)}, u32[]{:S(2)}) copy-start(pred[128,128]{1,0:T(8,128)(4,1)S(1)} %iota_compare_fusion) | copy-start | bytes 49156
  34.8 38.1 %copy-start.9 = (f32[128,128]{1,0:T(8,128)}, f32[128,128]{1,0:T(8,128)S(1)}, u32[]{:S(2)}) copy-start(f32[128,128]{1,0:T(8,128)S(1)} %fusion.54) | copy-start | bytes 196612
  46.6 26.5 %copy-start.11 = (f32[4096]{0:T(1024)S(1)}, f32[4096]{0:T(1024)}, u32[]{:S(2)}) copy-start(f32[4096]{0:T(1024)} %param.23) | copy-start | bytes 49156
  55.6 17.4 %copy-start.16 = (bf16[8,16]{1,0:T(8,128)(2,1)}, bf16[8,16]{1,0:T(8,128)(2,1)S(1)}, u32[]{:S(2)}) copy-start(bf16[8,16]{1,0:T(8,128)(2,1)S(1)} %get-tuple-element.436) | copy-start | bytes 772
  58.8 13.9 %all-to-all-start = ((bf16[4,32,1024]{2,1,0:T(8,128)(2,1)}), bf16[4,32,1024]{2,1,0:T(8,128)(2,1)S(1)}, u32[]{:S(2)}, u32[]{:S(2)}) async-start(bf16[4,32,1024]{2,1,0:T(8,128)(2,1)} %convert_element_type.138), calls=%async_computation | async-start | bytes 524288 | tf_op jit(solution)/shard_map/all_to_all | solution.py:160
  63.4 76.6 %all-gather.7.cloned.1.call-start = ((), (), s32[]{:S(2)}) async-start(), calls=%async_computation.5 | async-start | bytes 7077888 | tf_op jit(solution)/shard_map/all_gather | solution.py:90
  63.8 107.2 %copy-start.14 = (s32[64]{0:T(128)}, s32[64]{0:T(128)S(1)}, u32[]{:S(2)}) copy-start(s32[64]{0:T(128)S(1)} %multiply_add_fusion) | copy-start | bytes 772
  96.2 136.7 %reduce-scatter.2.cloned.1.call-start = ((), (), s32[]{:S(2)}) async-start(), calls=%async_computation.6 | async-start | bytes 7077888 | tf_op jit(solution)/shard_map/reduce_scatter | solution.py:95
  171.0 1.0 copy-start.2
  171.0 1.2 copy-start.8
  171.0 2.4 copy-start.17
  171.0 2.3 copy-start.15
  171.0 112.3 %copy-start.1 = (bf16[128,128]{1,0:T(8,128)(2,1)S(1)}, bf16[128,128]{1,0:T(8,128)(2,1)}, u32[]{:S(2)}) copy-start(bf16[128,128]{1,0:T(8,128)(2,1)} %param.18) | copy-start | bytes 98308
  171.0 112.3 %copy-start.6 = (f32[128,16]{0,1:T(8,128)S(1)}, f32[128,16]{0,1:T(8,128)}, u32[]{:S(2)}) copy-start(f32[128,16]{0,1:T(8,128)} %copy-done.5) | copy-start | bytes 24580
  171.1 92.3 %all-gather.11.cloned.1.call-start = ((), (), s32[]{:S(2)}) async-start(), calls=%async_computation.8 | async-start | bytes 2359296 | tf_op jit(solution)/shard_map/all_gather | solution.py:21
  172.1 111.6 %copy-start.4 = (f32[16,128]{1,0:T(8,128)S(1)}, f32[16,128]{1,0:T(8,128)}, u32[]{:S(2)}) copy-start(f32[16,128]{1,0:T(8,128)} %copy-done.3) | copy-start | bytes 24580
  172.1 111.6 %copy-start.10 = (f32[128,128]{1,0:T(8,128)S(1)}, f32[128,128]{1,0:T(8,128)}, u32[]{:S(2)}) copy-start(f32[128,128]{1,0:T(8,128)} %copy-done.9) | copy-start | bytes 196612
  172.1 111.6 %copy-start.13 = (pred[128,128]{1,0:T(8,128)(4,1)S(1)}, pred[128,128]{1,0:T(8,128)(4,1)}, u32[]{:S(2)}) copy-start(pred[128,128]{1,0:T(8,128)(4,1)} %copy-done.12) | copy-start | bytes 49156
  172.1 111.6 %copy-start.19 = (f32[16]{0:T(128)S(1)}, f32[16]{0:T(128)}, u32[]{:S(2)}) copy-start(f32[16]{0:T(128)} %param.21) | copy-start | bytes 196
  232.9 44.8 %all-to-all-start.2 = ((bf16[4,24,4096]{2,1,0:T(8,128)(2,1)}), bf16[4,24,4096]{2,1,0:T(8,128)(2,1)S(1)}, u32[]{:S(2)}, u32[]{:S(2)}) async-start(bf16[4,24,4096]{2,1,0:T(8,128)(2,1)} %bitcast.116), calls=%async_computation.3 | async-start | bytes 1572864 | tf_op jit(solution)/shard_map/all_to_all | solution.py:179
  278.7 13.9 %all-to-all-start.3 = ((bf16[32,4,1024]{2,0,1:T(8,128)(2,1)}), bf16[32,4,1024]{2,0,1:T(8,128)(2,1)S(1)}, u32[]{:S(2)}, u32[]{:S(2)}) async-start(bf16[32,4,1024]{2,0,1:T(8,128)(2,1)} %bitcast.95), calls=%async_computation.4 | async-start | bytes 524288 | tf_op jit(solution)/shard_map/all_to_all | solution.py:189
Sparse Core Ops, SparseCore 0:
  16.0 30.4 all-gather.8
  96.4 43.6 all-gather.6
  171.1 61.7 reduce-scatter.1
  235.4 27.8 all-gather.10
where the time goes:
time: 301 us; the launch traced here: 300 us
  waiting for transfers between devices  157 us (52%)
  matrix products  38.4 us (13%)
  blocking collectives  36.5 us (12%)
  other arithmetic  26.4 us (9%)
  starting transfers between devices  16.4 us (5%)
  between operations  14.9 us (5%)
  local copies, waits for them, and re-layouts  10.3 us (3%)
    reduce_scatter x1, waiting for transfers between devices, expert_block(): lax.psum_scatter(jnp.dot(hidden, down_local, preferred_element_type=jnp.f...  59.4 us
    all_gather x1, waiting for transfers between devices, expert_block(): lax.all_gather(rows_in, 'ctx', axis=0, tiled=True)  43.6 us
    all_gather x2, waiting for transfers between devices, prefix(): lax.all_gather(part.astype(kind), axis)  37.6 us
    dot_general x1, matrix products, expert_block(): jnp.dot(hidden, down_local, preferred_element_type=jnp.float32)  30.9 us
    all_to_all x1, blocking collectives, shards(): lax.all_to_all(outgoing.reshape(experts, most_rows, normed.shape[1]), 'ex...  22 us
    select_n x16, other arithmetic, turn(): return jax.tree.map(lambda a, b: jnp.where(reached, a, b), new, before)  17.5 us
    unnamed x1, blocking collectives  14.5 us
    all_to_all x1, waiting for transfers between devices, shards(): lax.all_to_all(ssd_out, 'exp', split_axis=0, concat_axis=1, tiled=True)  8.94 us
  transfers between devices with their start and end apart: 8, of which 6 were waited for; matrix products, arithmetic and copies ran while one was open for 8% of the time, Pallas kernels for 0%

commit v1 on v0

--- a/solution.py
+++ b/solution.py
@@ -186,7 +186,10 @@
     combined = gather_back(
         dispatch, returned.reshape(experts * most_rows, normed.shape[1]), my_weights
     )
-    moe_out = lax.all_to_all(combined, "exp", split_axis=1, concat_axis=0, tiled=True)
+    moe_out = jnp.concatenate(
+        lax.all_to_all(jnp.stack(jnp.split(combined, lax.axis_size("exp"), axis=1)), "exp", 0, 0),
+        axis=0,
+    )
     return (moe_out, grad_conv)
 
 

time: 301 us -> 301 us (level)
  no operation moved by 1% of the time
where the time goes in v1:
time: 301 us; the launch traced here: 300 us
  waiting for transfers between devices  157 us (52%)
  matrix products  38.3 us (13%)
  blocking collectives  36.5 us (12%)
  other arithmetic  26.8 us (9%)
  starting transfers between devices  16.4 us (5%)
  between operations  14.9 us (5%)
  local copies, waits for them, and re-layouts  9.58 us (3%)
    reduce_scatter x1, waiting for transfers between devices, expert_block(): lax.psum_scatter(jnp.dot(hidden, down_local, preferred_element_type=jnp.f...  59.5 us
    all_gather x1, waiting for transfers between devices, expert_block(): lax.all_gather(rows_in, 'ctx', axis=0, tiled=True)  43.6 us
    all_gather x2, waiting for transfers between devices, prefix(): lax.all_gather(part.astype(kind), axis)  37.6 us
    dot_general x1, matrix products, expert_block(): jnp.dot(hidden, down_local, preferred_element_type=jnp.float32)  30.9 us
    all_to_all x1, blocking collectives, shards(): lax.all_to_all(outgoing.reshape(experts, most_rows, normed.shape[1]), 'ex...  22 us
    select_n x16, other arithmetic, turn(): return jax.tree.map(lambda a, b: jnp.where(reached, a, b), new, before)  17.5 us
    unnamed x1, blocking collectives  14.5 us
    all_to_all x1, waiting for transfers between devices, shards(): lax.all_to_all(ssd_out, 'exp', split_axis=0, concat_axis=1, tiled=True)  8.94 us
  transfers between devices with their start and end apart: 8, of which 6 were waited for; matrix products, arithmetic and copies ran while one was open for 8% of the time, Pallas kernels for 0%

profile of v1, /device:TPU:0, one launch (start us, length us, event | category | flops | bytes accessed | tf_op | source)
XLA Modules:
  0.0 299.6 jit_solution(188655138731517141)
XLA Ops:
  7.2 0.7 slice.29
  8.0 2.3 collective-permute-start
  10.3 0.9 fusion.53
  11.2 1.0 reduce_window_sum.23
  12.5 1.0 convert_element_type.128
  13.5 0.3 multiply_convert_fusion.2
  14.0 1.9 convolution_convert_fusion.2
  15.9 1.2 dynamic-slice
  18.0 0.2 dynamic-update-slice
  18.3 14.5 %all-reduce = bf16[128]{0:T(256)(128)(2,1)S(1)} all-reduce(bf16[128]{0:T(256)(128)(2,1)S(1)} %dynamic-update-slice), channel_id=2, replica_groups=mesh['ctx'=8,'exp'=4] {'ctx'}, use_global_device_ids=true, to_apply=%add | all-reduce | flops 128 | bytes 512
  32.8 0.8 constant_dynamic-slice_fusion
  33.8 0.9 fusion.54
  34.8 11.8 %all-gather.9.cloned.1.call-done = bf16[128,64,128]{2,1,0:T(8,128)(2,1)} async-done(((bf16[16,64,128]{2,1,0:T(8,128)(2,1)}), bf16[128,64,128]{2,1,0:T(8,128)(2,1)}) %all-gather.9.cloned.1.call-update) | async-done | bytes 2097168 | tf_op jit(solution)/shard_map/all_gather | solution.py:21
  46.6 9.1 %while.30 = (s32[]{:T(128)}, f32[16,64,128]{2,1,0:T(8,128)S(1)}, s32[]{:T(128)}, bf16[8,16]{1,0:T(8,128)(2,1)S(1)}, bf16[8,16,64,128]{3,2,1,0:T(8,128)(2,1)}, /*index=5*/s32[]{:T(128)}, s32[]{:T(128)}) while((s32[]{:T(128)}, f32[16,64,128]{2,1,0:T(8,128)S(1)}, s32[]{:T(128)}, bf16[8,16]{1,0:T(8,128)(2,1)S(1)}, ...), condition=%wide.region_4.5_spmd.clone, body=%wide.region_3.4_spmd.clone.sunk | while | flops 655380 | bytes 1310985 | solution.py:35
  46.6 1.1 fusion.66
  47.7 1.1 fusion.66
  48.8 1.1 fusion.66
  50.0 1.1 fusion.66
  51.1 1.1 fusion.66
  52.3 1.1 fusion.66
  53.4 1.1 fusion.66
  54.5 1.1 fusion.66
  55.6 0.4 fusion.18
  56.0 1.3 fusion.20
  57.4 0.4 copy.27
  57.8 1.1 convert_element_type.134
  58.8 4.6 %all-to-all-start = ((bf16[4,32,1024]{2,1,0:T(8,128)(2,1)}), bf16[4,32,1024]{2,1,0:T(8,128)(2,1)S(1)}, u32[]{:S(2)}, u32[]{:S(2)}) async-start(bf16[4,32,1024]{2,1,0:T(8,128)(2,1)} %convert_element_type.134), calls=%async_computation | async-start | bytes 524288 | tf_op jit(solution)/shard_map/all_to_all | solution.py:160
  63.8 8.9 %all-to-all-done = bf16[4,32,1024]{2,1,0:T(8,128)(2,1)S(1)} async-done(((bf16[4,32,1024]{2,1,0:T(8,128)(2,1)}), bf16[4,32,1024]{2,1,0:T(8,128)(2,1)S(1)}, u32[]{:S(2)}, u32[]{:S(2)}) %all-to-all-start) | async-done | bytes 262176 | tf_op jit(solution)/shard_map/all_to_all | solution.py:160
  73.2 0.5 broadcast_in_dim.50
  73.9 0.3 convolution_convert_fusion
  74.2 22.0 %all_to_all.25 = bf16[4,24,4096]{2,1,0:T(8,128)(2,1)} all-to-all(bf16[4,24,4096]{2,1,0:T(8,128)(2,1)S(1)} %bitcast.108), channel_id=1, replica_groups=mesh['ctx'=8,'exp'=4] {'exp'}, dimensions={0} | all-to-all | bytes 1572864 | tf_op jit(solution)/shard_map/all_to_all | solution.py:169
  96.2 0.2 reduce-scatter.2.cloned.1.call-start
  96.5 43.6 %all-gather.7.cloned.1.call-done = bf16[768,4096]{1,0:T(8,128)(2,1)} async-done(((bf16[96,4096]{1,0:T(8,128)(2,1)}), bf16[768,4096]{1,0:T(8,128)(2,1)}) %all-gather.7.cloned.1.call-update) | async-done | bytes 6291472 | tf_op jit(solution)/shard_map/all_gather | solution.py:90
  140.1 30.9 %fusion.6 = bf16[768,4096]{1,0:T(8,128)(2,1)} fusion(bf16[1,1536,4096]{2,1,0:T(8,128)(2,1)} %param.27, bf16[768,4096]{1,0:T(8,128)(2,1)} %all-gather.7.cloned.1.call-done, bf16[1,4096,1536]{2,1,0:T(8,128)(2,1)} %param.26), kind=kOutput, calls=%fused_computation.10 | convolution fusion | flops 19336396800 | bytes 37748736 | tf_op jit(solution)/shard_map/dot_general | solution.py:96
  171.1 0.8 copy-done.2
  172.1 1.1 convolution_convert_fusion.1
  173.5 59.5 %reduce-scatter.2.cloned.1.call-done = bf16[96,4096]{1,0:T(8,128)(2,1)} async-done(((bf16[768,4096]{1,0:T(8,128)(2,1)}), bf16[96,4096]{1,0:T(8,128)(2,1)}) %reduce-scatter.2.cloned.1.call-update) | async-done | bytes 786448 | tf_op jit(solution)/shard_map/reduce_scatter | solution.py:95
  232.9 4.6 %all-to-all-start.2 = ((bf16[4,24,4096]{2,1,0:T(8,128)(2,1)}), bf16[4,24,4096]{2,1,0:T(8,128)(2,1)S(1)}, u32[]{:S(2)}, u32[]{:S(2)}) async-start(bf16[4,24,4096]{2,1,0:T(8,128)(2,1)} %bitcast.117), calls=%async_computation.3 | async-start | bytes 1572864 | tf_op jit(solution)/shard_map/all_to_all | solution.py:179
  237.5 25.8 %all-gather.11.cloned.1.call-done = bf16[128,64,128]{2,1,0:T(8,128)(2,1)} async-done(((bf16[16,64,128]{2,1,0:T(8,128)(2,1)}), bf16[128,64,128]{2,1,0:T(8,128)(2,1)}) %all-gather.11.cloned.1.call-update) | async-done | bytes 2097168 | tf_op jit(solution)/shard_map/all_gather | solution.py:21
  263.3 14.1 %while.31 = (s32[]{:T(128)}, f32[16,64,128]{2,1,0:T(8,128)S(1)}, s32[]{:T(128)}, bf16[8,16]{1,0:T(8,128)(2,1)}, bf16[8,16,64,128]{3,2,1,0:T(8,128)(2,1)}, /*index=5*/s32[]{:T(128)}, s32[]{:T(128)}, s32[]{:T(128)}, s32[]{:T(128)}) while((s32[]{:T(128)}, f32[16,64,128]{2,1,0:T(8,128)S(1)}, s32[]{:T(128)}, bf16[8,16]{1,0:T(8,128)(2,1)}, ...), condition=%wide.region_9.10_spmd.clone, body=%wide.region_8.9_spmd.clone.sunk | while | flops 655384 | bytes 1311047 | solution.py:35
  263.3 0.6 bitcast_convert_fusion.5
  264.0 1.1 fusion.67
  265.1 0.6 bitcast_convert_fusion.5
  265.7 1.1 fusion.67
  266.8 0.6 bitcast_convert_fusion.5
  267.5 1.1 fusion.67
  268.6 0.6 bitcast_convert_fusion.5
  269.2 1.1 fusion.67
  270.4 0.6 bitcast_convert_fusion.5
  271.0 1.1 fusion.67
  272.1 0.6 bitcast_convert_fusion.5
  272.8 1.1 fusion.67
  273.9 0.6 bitcast_convert_fusion.5
  274.5 1.1 fusion.67
  275.6 0.6 bitcast_convert_fusion.5
  276.3 1.1 fusion.67
  277.4 0.3 fusion.13
  277.7 0.7 pad_maximum_fusion.1
  278.5 4.6 %all-to-all-start.3 = ((bf16[4,32,1024]{2,1,0:T(8,128)(2,1)}), bf16[4,32,1024]{2,1,0:T(8,128)(2,1)S(1)}, u32[]{:S(2)}, u32[]{:S(2)}) async-start(bf16[4,32,1024]{2,1,0:T(8,128)(2,1)} %pad_maximum_fusion.1), calls=%async_computation.4 | async-start | bytes 524288 | tf_op jit(solution)/shard_map/all_to_all | solution.py:190
  283.1 0.4 fusion.19
  283.5 0.9 fusion.15
  284.4 1.0 copy.31
  285.4 7.0 %all-to-all-done.3 = bf16[4,32,1024]{2,1,0:T(8,128)(2,1)S(1)} async-done(((bf16[4,32,1024]{2,1,0:T(8,128)(2,1)}), bf16[4,32,1024]{2,1,0:T(8,128)(2,1)S(1)}, u32[]{:S(2)}, u32[]{:S(2)}) %all-to-all-start.3) | async-done | bytes 262176 | tf_op jit(solution)/shard_map/all_to_all | solution.py:190
  292.4 0.7 copy.49
  (83 shorter events, 2.5 us)
Async XLA Ops:
  7.2 26.7 %copy-start = (bf16[128,128]{1,0:T(8,128)(2,1)S(1)}, bf16[128,128]{1,0:T(8,128)(2,1)}, u32[]{:S(2)}) copy-start(bf16[128,128]{1,0:T(8,128)(2,1)} %param.19) | copy-start | bytes 98308
  7.2 48.9 %copy-start.18 = (f32[16]{0:T(128)S(1)}, f32[16]{0:T(128)}, u32[]{:S(2)}) copy-start(f32[16]{0:T(128)} %param.21) | copy-start | bytes 196
  7.2 39.4 %all-gather.9.cloned.1.call-start = ((), (), s32[]{:S(2)}) async-start(), calls=%async_computation.7 | async-start | bytes 2359296 | tf_op jit(solution)/shard_map/all_gather | solution.py:21
  8.0 5.5 %collective-permute-start = (bf16[3,1024]{1,0:T(4,128)(2,1)S(1)}, bf16[3,1024]{1,0:T(4,128)(2,1)S(1)}, u32[]{:S(2)}, u32[]{:S(2)}) collective-permute-start(bf16[3,1024]{1,0:T(4,128)(2,1)S(1)} %slice.29), channel_id=1, source_target_pairs={{0,4},{4,8},{8,12},{12,16},{16,20},{20,24},{24,28},{1,5},{5,9},{9,... | collective-permute-start | bytes 18440 | tf_op jit(solution)/shard_map/ppermute | solution.py:15
  12.2 45.1 %copy-start.3 = (f32[16,128]{1,0:T(8,128)}, f32[16,128]{1,0:T(8,128)S(1)}, u32[]{:S(2)}) copy-start(f32[16,128]{1,0:T(8,128)S(1)} %reduce_window_sum.23) | copy-start | bytes 24580
  12.4 3.5 %copy-start.5 = (f32[128,16]{0,1:T(8,128)}, f32[128,16]{0,1:T(8,128)S(1)}, u32[]{:S(2)}) copy-start(f32[128,16]{0,1:T(8,128)S(1)} %get-tuple-element.301) | copy-start | bytes 24580
  12.4 44.9 %copy-start.7 = (f32[128,16]{0,1:T(8,128)}, f32[128,16]{0,1:T(8,128)S(1)}, u32[]{:S(2)}) copy-start(f32[128,16]{0,1:T(8,128)S(1)} %get-tuple-element.300) | copy-start | bytes 24580
  33.8 29.8 %copy-start.12 = (pred[128,128]{1,0:T(8,128)(4,1)}, pred[128,128]{1,0:T(8,128)(4,1)S(1)}, u32[]{:S(2)}) copy-start(pred[128,128]{1,0:T(8,128)(4,1)S(1)} %iota_compare_fusion) | copy-start | bytes 49156
  34.8 38.1 %copy-start.9 = (f32[128,128]{1,0:T(8,128)}, f32[128,128]{1,0:T(8,128)S(1)}, u32[]{:S(2)}) copy-start(f32[128,128]{1,0:T(8,128)S(1)} %fusion.54) | copy-start | bytes 196612
  46.6 26.5 %copy-start.11 = (f32[4096]{0:T(1024)S(1)}, f32[4096]{0:T(1024)}, u32[]{:S(2)}) copy-start(f32[4096]{0:T(1024)} %param.23) | copy-start | bytes 49156
  55.6 17.4 %copy-start.16 = (bf16[8,16]{1,0:T(8,128)(2,1)}, bf16[8,16]{1,0:T(8,128)(2,1)S(1)}, u32[]{:S(2)}) copy-start(bf16[8,16]{1,0:T(8,128)(2,1)S(1)} %get-tuple-element.438) | copy-start | bytes 772
  58.8 13.9 %all-to-all-start = ((bf16[4,32,1024]{2,1,0:T(8,128)(2,1)}), bf16[4,32,1024]{2,1,0:T(8,128)(2,1)S(1)}, u32[]{:S(2)}, u32[]{:S(2)}) async-start(bf16[4,32,1024]{2,1,0:T(8,128)(2,1)} %convert_element_type.134), calls=%async_computation | async-start | bytes 524288 | tf_op jit(solution)/shard_map/all_to_all | solution.py:160
  63.4 76.6 %all-gather.7.cloned.1.call-start = ((), (), s32[]{:S(2)}) async-start(), calls=%async_computation.5 | async-start | bytes 7077888 | tf_op jit(solution)/shard_map/all_gather | solution.py:90
  63.8 107.2 %copy-start.14 = (s32[64]{0:T(128)}, s32[64]{0:T(128)S(1)}, u32[]{:S(2)}) copy-start(s32[64]{0:T(128)S(1)} %multiply_add_fusion) | copy-start | bytes 772
  96.2 136.7 %reduce-scatter.2.cloned.1.call-start = ((), (), s32[]{:S(2)}) async-start(), calls=%async_computation.6 | async-start | bytes 7077888 | tf_op jit(solution)/shard_map/reduce_scatter | solution.py:95
  171.0 1.0 copy-start.2
  171.0 1.1 copy-start.8
  171.0 2.4 copy-start.17
  171.0 2.3 copy-start.15
  171.0 112.0 %copy-start.1 = (bf16[128,128]{1,0:T(8,128)(2,1)S(1)}, bf16[128,128]{1,0:T(8,128)(2,1)}, u32[]{:S(2)}) copy-start(bf16[128,128]{1,0:T(8,128)(2,1)} %param.18) | copy-start | bytes 98308
  171.0 112.0 %copy-start.6 = (f32[128,16]{0,1:T(8,128)S(1)}, f32[128,16]{0,1:T(8,128)}, u32[]{:S(2)}) copy-start(f32[128,16]{0,1:T(8,128)} %copy-done.5) | copy-start | bytes 24580
  171.1 92.3 %all-gather.11.cloned.1.call-start = ((), (), s32[]{:S(2)}) async-start(), calls=%async_computation.8 | async-start | bytes 2359296 | tf_op jit(solution)/shard_map/all_gather | solution.py:21
  173.2 110.2 %copy-start.4 = (f32[16,128]{1,0:T(8,128)S(1)}, f32[16,128]{1,0:T(8,128)}, u32[]{:S(2)}) copy-start(f32[16,128]{1,0:T(8,128)} %copy-done.3) | copy-start | bytes 24580
  173.2 110.3 %copy-start.10 = (f32[128,128]{1,0:T(8,128)S(1)}, f32[128,128]{1,0:T(8,128)}, u32[]{:S(2)}) copy-start(f32[128,128]{1,0:T(8,128)} %copy-done.9) | copy-start | bytes 196612
  173.2 110.3 %copy-start.13 = (pred[128,128]{1,0:T(8,128)(4,1)S(1)}, pred[128,128]{1,0:T(8,128)(4,1)}, u32[]{:S(2)}) copy-start(pred[128,128]{1,0:T(8,128)(4,1)} %copy-done.12) | copy-start | bytes 49156
  173.2 110.3 %copy-start.19 = (f32[16]{0:T(128)S(1)}, f32[16]{0:T(128)}, u32[]{:S(2)}) copy-start(f32[16]{0:T(128)} %param.21) | copy-start | bytes 196
  232.9 44.5 %all-to-all-start.2 = ((bf16[4,24,4096]{2,1,0:T(8,128)(2,1)}), bf16[4,24,4096]{2,1,0:T(8,128)(2,1)S(1)}, u32[]{:S(2)}, u32[]{:S(2)}) async-start(bf16[4,24,4096]{2,1,0:T(8,128)(2,1)} %bitcast.117), calls=%async_computation.3 | async-start | bytes 1572864 | tf_op jit(solution)/shard_map/all_to_all | solution.py:179
  278.5 13.9 %all-to-all-start.3 = ((bf16[4,32,1024]{2,1,0:T(8,128)(2,1)}), bf16[4,32,1024]{2,1,0:T(8,128)(2,1)S(1)}, u32[]{:S(2)}, u32[]{:S(2)}) async-start(bf16[4,32,1024]{2,1,0:T(8,128)(2,1)} %pad_maximum_fusion.1), calls=%async_computation.4 | async-start | bytes 524288 | tf_op jit(solution)/shard_map/all_to_all | solution.py:190
Sparse Core Ops, SparseCore 0:
  16.0 30.4 all-gather.8
  96.4 43.6 all-gather.6
  171.1 61.7 reduce-scatter.1
  235.4 27.8 all-gather.10
